TPU v7x, 32 devices: a whole 2x2x4 slice. The times are simulated.
32 devices in a mesh: dp: 16 (over z, y, core), tensor: 2 (over x).
Axes of the slice: x: 2, y: 2, z: 4, core: 2. Of those that a mesh axis runs over, the one named last changes fastest.
Arguments:
- tokens: float32 [16384, 1024], P(('dp', 'tensor')), may hold values from -6 to 6
- norm_gain: float32 [1024], P(('dp', 'tensor')), may hold values from 0.5 to 1.5
- w_z: bfloat16 [1024, 2048], P('dp', 'tensor'), may hold values from -0.1875 to 0.1875
- w_x: bfloat16 [1024, 2048], P('dp', 'tensor'), may hold values from -0.1875 to 0.1875
- w_dt: bfloat16 [1024, 32], P('dp', 'tensor'), may hold values from -0.1875 to 0.1875
- w_bc: bfloat16 [1024, 256], P(('dp', 'tensor')), may hold values from -0.1875 to 0.1875
- w_out: bfloat16 [1024, 2048], P('dp', 'tensor'), may hold values from -0.125 to 0.125
- conv_x_w: float32 [2048, 4], P('tensor'), may hold values from -3 to 3
- conv_x_b: float32 [2048], P('tensor'), may hold values from -0.5 to 0.5
- conv_bc_w: float32 [256, 4], P(('dp', 'tensor')), may hold values from -3 to 3
- conv_bc_b: float32 [256], P(('dp', 'tensor')), may hold values from -0.5 to 0.5
- a_log: float32 [32], P('tensor'), may hold values from -1 to 1.5
- d_skip: float32 [32], P('tensor'), may hold values from 0.5 to 1.5
- dt_bias: float32 [32], P('tensor'), may hold values from -7 to -2.5
- norm_w: float32 [2048], P('tensor'), may hold values from 0.5 to 1.5
- block_seq: int32 [64], P('dp'), may hold values from 0 to 63, as said below
- block_len: int32 [64], P('dp'), may hold values from 0 to 256, as said below
- cotangent: float32 [16384, 1024], P(('dp', 'tensor')), may hold values from -6 to 6
Outputs:
- output: float32 [16384, 1024], P(('dp', 'tensor'))
- d_tokens: float32 [16384, 1024], P(('dp', 'tensor'))
- d_gain: float32 [1024], P(('dp', 'tensor'))
- d_w_z: float32 [1024, 2048], P('dp', 'tensor')
- d_w_x: float32 [1024, 2048], P('dp', 'tensor')
- d_w_dt: float32 [1024, 32], P('dp', 'tensor')
- d_w_bc: float32 [1024, 256], P(('dp', 'tensor'))
- d_w_out: float32 [1024, 2048], P('dp', 'tensor')
- d_conv_x_w: float32 [2048, 4], P('tensor')
- d_conv_x_b: float32 [2048], P('tensor')
- d_conv_bc_w: float32 [256, 4], P(('dp', 'tensor'))
- d_conv_bc_b: float32 [256], P(('dp', 'tensor'))
- d_a_log: float32 [32], P('tensor')
- d_d_skip: float32 [32], P('tensor')
- d_dt_bias: float32 [32], P('tensor')
- d_norm_w: float32 [2048], P('tensor')
Inputs may be any that keep to these rules, and one draw needn't show every extreme that they name: `block_seq`: each index of dp holds 4 slots; a sequence takes consecutive slots of one index starting at a slot's first row, every slot but its last full; adjacent slots of one index carry the same value exactly when they hold one sequence; an empty slot has a value no other slot has. `block_len`: rows in use count from a slot's start; an empty slot has 0; fewer than 256 only in a sequence's last slot.
All inputs are finite; a program needn't handle non-finite values.
Results may differ from a plain program's by a relative error of at most 0.0082.
Values may be sent and summed in bfloat16 or wider, within the bound.
A program may use at most 192 MiB of HBM per device.

v0:
```python
import jax
import jax.numpy as jnp
from jax import lax
from jax.sharding import PartitionSpec as P

INNER = 2048
HEADDIM = 64
STATE = 128
BLOCK = 256
EPSILON = 1e-05
HIGHEST_PREC = lax.Precision.HIGHEST


def shift_rows(values, lag_rows):
    if lag_rows == 0:
        return values
    zero_rows = jnp.zeros((lag_rows,) + values.shape[1:], values.dtype)
    return jnp.concatenate([zero_rows, values[:-lag_rows]], axis=0)


def causal_conv(values, weights, bias_vec, keep_masks):
    taps_count = weights.shape[1]
    summed = jnp.zeros_like(values) + bias_vec[None, :]
    for offset in range(taps_count):
        lag_rows = taps_count - 1 - offset
        shifted = shift_rows(values, lag_rows) * keep_masks[lag_rows][:, None]
        summed = summed + shifted * weights[:, offset][None, :]
    return jax.nn.silu(summed)


def scan_heads(
    x_pre,
    bc_pre,
    dt_raw,
    conv_x_w,
    conv_x_b,
    conv_bc_w,
    conv_bc_b,
    a_log,
    d_skip,
    dt_bias,
    carry_flags,
    token_mask,
):
    row_count = x_pre.shape[0]
    slot_count = row_count // BLOCK
    head_count = dt_raw.shape[1]
    position = jnp.arange(row_count) % BLOCK
    carry_rows = jnp.repeat(carry_flags, BLOCK)
    keep_masks = [
        jnp.where(position >= lag_rows, jnp.ones_like(carry_rows), carry_rows)
        for lag_rows in range(conv_x_w.shape[1])
    ]
    x_conv = causal_conv(x_pre, conv_x_w, conv_x_b, keep_masks)
    bc_conv = causal_conv(bc_pre, conv_bc_w, conv_bc_b, keep_masks)
    state_in = bc_conv[:, :STATE].reshape(slot_count, BLOCK, STATE)
    state_out = bc_conv[:, STATE:].reshape(slot_count, BLOCK, STATE)
    inputs = x_conv.reshape(slot_count, BLOCK, head_count, HEADDIM)
    steps_dt = jax.nn.softplus(dt_raw + dt_bias[None, :]) * token_mask[:, None]
    decay_rates = (steps_dt * (-jnp.exp(a_log))[None, :]).reshape(slot_count, BLOCK, head_count)
    steps_three = steps_dt.reshape(slot_count, BLOCK, head_count)
    lower_mask = (jnp.arange(BLOCK)[:, None] >= jnp.arange(BLOCK)[None, :]).astype(x_pre.dtype)
    cumulative = jnp.einsum("ij,sjh->sih", lower_mask, decay_rates, precision=HIGHEST_PREC)
    scores_cb = jnp.einsum("sin,sjn->sij", state_out, state_in, precision=HIGHEST_PREC)
    differ = cumulative[:, :, None, :] - cumulative[:, None, :, :]
    decay_mat = jnp.exp(jnp.where(lower_mask[None, :, :, None] > 0.5, differ, -1e30))
    mixing = scores_cb[:, :, :, None] * decay_mat * steps_three[:, None, :, :]
    y_local = jnp.einsum("sijh,sjhp->sihp", mixing, inputs, precision=HIGHEST_PREC)
    span_total = cumulative[:, -1, :]
    to_end = jnp.exp(span_total[:, None, :] - cumulative) * steps_three
    block_states = jnp.einsum(
        "sjn,sjh,sjhp->shnp", state_in, to_end, inputs, precision=HIGHEST_PREC
    )
    carried = []
    current = jnp.zeros((head_count, STATE, HEADDIM), x_pre.dtype)
    for slot_index in range(slot_count):
        current = current * carry_flags[slot_index]
        carried.append(current)
        current = (
            current * jnp.exp(span_total[slot_index])[:, None, None] + block_states[slot_index]
        )
    entering = jnp.stack(carried)
    y_state = (
        jnp.einsum("sin,shnp->sihp", state_out, entering, precision=HIGHEST_PREC)
        * jnp.exp(cumulative)[:, :, :, None]
    )
    output = y_local + y_state + inputs * d_skip[None, None, :, None]
    return output.reshape(row_count, head_count * HEADDIM)


def dot_nt(left, right):
    return lax.dot_general(
        left, right, (((1,), (1,)), ((), ())), preferred_element_type=jnp.float32
    )


def dot_tn(left, right):
    return lax.dot_general(
        left, right, (((0,), (0,)), ((), ())), preferred_element_type=jnp.float32
    )


def per_device(
    tokens,
    norm_gain,
    w_z,
    w_x,
    w_dt,
    w_bc,
    w_out,
    conv_x_w,
    conv_x_b,
    conv_bc_w,
    conv_bc_b,
    a_log,
    d_skip,
    dt_bias,
    norm_w,
    block_seq,
    block_len,
    cotangent,
):
    bc_full, gain_full, conv_bcw_full, conv_bcb_full = (
        lax.all_gather(w_bc.astype(jnp.float32), ("dp", "tensor"), axis=0, tiled=True),
        lax.all_gather(norm_gain, ("dp", "tensor"), axis=0, tiled=True),
        lax.all_gather(conv_bc_w, ("dp", "tensor"), axis=0, tiled=True),
        lax.all_gather(conv_bc_b, ("dp", "tensor"), axis=0, tiled=True),
    )
    bc_weight = bc_full.astype(jnp.bfloat16)
    mean_sq = jnp.mean(tokens * tokens, axis=1, keepdims=True)
    inv_rms = lax.rsqrt(mean_sq + EPSILON)
    unit_rows = tokens * inv_rms
    normed_own = (unit_rows * gain_full[None, :]).astype(jnp.bfloat16)
    normed = lax.all_gather(normed_own, "tensor", axis=0, tiled=True)
    z_full, x_full, dt_full, out_full = (
        lax.all_gather(w_z, "dp", axis=0, tiled=True),
        lax.all_gather(w_x, "dp", axis=0, tiled=True),
        lax.all_gather(w_dt, "dp", axis=0, tiled=True),
        lax.all_gather(w_out, "dp", axis=0, tiled=True),
    )
    row_count = normed.shape[0]
    slot_count = block_seq.shape[0]
    slot_index = jnp.arange(slot_count)
    previous = jnp.concatenate([block_seq[:1] - 1, block_seq[:-1]])
    carry_flags = ((slot_index > 0) & (block_seq == previous)).astype(jnp.float32)
    token_mask = (jnp.arange(row_count) % BLOCK < jnp.repeat(block_len, BLOCK)).astype(jnp.float32)
    gate_pre = jnp.dot(normed, z_full, preferred_element_type=jnp.float32)
    x_pre = jnp.dot(normed, x_full, preferred_element_type=jnp.float32)
    bc_pre = jnp.dot(normed, bc_weight, preferred_element_type=jnp.float32)
    dt_raw = jnp.dot(normed, dt_full, preferred_element_type=jnp.float32)

    def local_scan(xp_in, bc_in, dt_in, cxw, cxb, cbw, cbb, alog_in, skip_in, bias_in):
        return scan_heads(
            xp_in,
            bc_in,
            dt_in,
            cxw,
            cxb,
            cbw,
            cbb,
            alog_in,
            skip_in,
            bias_in,
            carry_flags,
            token_mask,
        )

    y_local, scan_back = jax.vjp(
        local_scan,
        x_pre,
        bc_pre,
        dt_raw,
        conv_x_w,
        conv_x_b,
        conv_bcw_full,
        conv_bcb_full,
        a_log,
        d_skip,
        dt_bias,
    )
    gated_rows = y_local * jax.nn.silu(gate_pre)
    sq_sum = lax.psum(jnp.sum(gated_rows * gated_rows, axis=1), "tensor")
    inv_g = lax.rsqrt(sq_sum[:, None] / INNER + EPSILON)
    unit_g = gated_rows * inv_g
    hidden = (unit_g * norm_w[None, :] * token_mask[:, None]).astype(jnp.bfloat16)
    branch = lax.psum_scatter(
        dot_nt(hidden, out_full).astype(jnp.bfloat16), "tensor", scatter_dimension=0, tiled=True
    ).astype(jnp.float32)
    output = tokens + branch
    cot_rows = lax.all_gather(cotangent.astype(jnp.bfloat16), "tensor", axis=0, tiled=True)
    z_back, x_back, dt_back, out_back = (z_full, x_full, dt_full, out_full)
    d_hidden = jnp.dot(cot_rows, out_back, preferred_element_type=jnp.float32)
    g_w_out = lax.psum_scatter(dot_tn(cot_rows, hidden), "dp", scatter_dimension=0, tiled=True)
    d_unit = d_hidden * norm_w[None, :] * token_mask[:, None]
    g_norm_w = jnp.sum(d_hidden * unit_g * token_mask[:, None], axis=0)
    inner_sum = lax.psum(jnp.sum(d_unit * unit_g, axis=1), "tensor")
    d_gated = inv_g * (d_unit - unit_g * inner_sum[:, None] / INNER)
    sigmoid_gate = jax.nn.sigmoid(gate_pre)
    d_y = d_gated * gate_pre * sigmoid_gate
    d_gate = d_gated * y_local * sigmoid_gate * (1.0 + gate_pre * (1.0 - sigmoid_gate))
    d_xp, d_bc, d_dt, g_cxw, g_cxb, g_cbw, g_cbb, g_alog, g_skip, g_bias = scan_back(d_y)
    gate_g = d_gate.astype(jnp.bfloat16)
    x_g = d_xp.astype(jnp.bfloat16)
    dt_g = d_dt.astype(jnp.bfloat16)
    bc_g = d_bc.astype(jnp.bfloat16)
    joined = jnp.concatenate([gate_g, x_g, dt_g], axis=1)
    in_grads = lax.psum_scatter(dot_tn(normed, joined), "dp", scatter_dimension=0, tiled=True)
    width_local = w_z.shape[1]
    g_w_z = in_grads[:, :width_local]
    g_w_x = in_grads[:, width_local : 2 * width_local]
    g_w_dt = in_grads[:, 2 * width_local :]
    g_w_bc_part = dot_tn(normed, bc_g)
    summed = dot_nt(gate_g, z_back) + dot_nt(x_g, x_back)
    d_normed = lax.psum_scatter(
        summed + dot_nt(dt_g, dt_back) + dot_nt(bc_g, bc_weight),
        "tensor",
        scatter_dimension=0,
        tiled=True,
    )
    g_gain_part = jnp.sum(d_normed * unit_rows, axis=0)
    d_unit_r = d_normed * gain_full[None, :]
    d_tokens = cotangent + inv_rms * (
        d_unit_r - unit_rows * jnp.mean(d_unit_r * unit_rows, axis=1, keepdims=True)
    )
    g_w_bc, g_gain, g_conv_bcw, g_conv_bcb = (
        lax.psum_scatter(g_w_bc_part, ("dp", "tensor"), scatter_dimension=0, tiled=True),
        lax.psum_scatter(g_gain_part, ("dp", "tensor"), scatter_dimension=0, tiled=True),
        lax.psum_scatter(g_cbw, ("dp", "tensor"), scatter_dimension=0, tiled=True),
        lax.psum_scatter(g_cbb, ("dp", "tensor"), scatter_dimension=0, tiled=True),
    )
    g_cxw, g_cxb, g_alog, g_skip, g_bias, g_norm_w = lax.psum(
        (g_cxw, g_cxb, g_alog, g_skip, g_bias, g_norm_w), "dp"
    )
    return (
        output,
        d_tokens,
        g_gain,
        g_w_z,
        g_w_x,
        g_w_dt,
        g_w_bc,
        g_w_out,
        g_cxw,
        g_cxb,
        g_conv_bcw,
        g_conv_bcb,
        g_alog,
        g_skip,
        g_bias,
        g_norm_w,
    )


def solution(mesh):
    return jax.shard_map(
        per_device,
        mesh=mesh,
        in_specs=(
            P(("dp", "tensor"), None),
            P(("dp", "tensor")),
            P("dp", "tensor"),
            P("dp", "tensor"),
            P("dp", "tensor"),
            P(("dp", "tensor"), None),
            P("dp", "tensor"),
            P("tensor", None),
            P("tensor"),
            P(("dp", "tensor"), None),
            P(("dp", "tensor")),
            P("tensor"),
            P("tensor"),
            P("tensor"),
            P("tensor"),
            P("dp"),
            P("dp"),
            P(("dp", "tensor"), None),
        ),
        out_specs=(
            P(("dp", "tensor"), None),
            P(("dp", "tensor"), None),
            P(("dp", "tensor")),
            P("dp", "tensor"),
            P("dp", "tensor"),
            P("dp", "tensor"),
            P(("dp", "tensor"), None),
            P("dp", "tensor"),
            P("tensor", None),
            P("tensor"),
            P(("dp", "tensor"), None),
            P(("dp", "tensor")),
            P("tensor"),
            P("tensor"),
            P("tensor"),
            P("tensor"),
        ),
        check_vma=False,
    )
```

profile of v0, /device:TPU:0, one launch (start us, length us, event | category | flops | bytes accessed | tf_op | source)
XLA Modules:
  0.0 878.6 jit_solution(2588290233400417949)
XLA Ops:
  7.3 1.9 multiply_reduce_fusion.13
  10.9 42.0 %all-reduce.35 = (f32[1024]{0:T(1024)S(1)}, f32[256]{0:T(256)}) all-reduce(f32[1024]{0:T(1024)S(1)} %dynamic-update-slice, f32[256]{0:T(256)S(1)} %dynamic-update-slice.1), channel_id=1, replica_groups=mesh['dp'=16,'tensor'=2] {'dp','tensor'}, use_global_device_ids=true, to_apply=%add.29 | all-reduce | flops 1280 | bytes 10240
  53.0 2.9 multiply_convert_fusion.2
  60.5 21.4 %all-gather.1 = bf16[16,64,16]{1,2,0:T(8,128)(2,1)S(1)} all-gather(bf16[1,64,16]{1,2,0:T(8,128)(2,1)S(1)} %bitcast.308), channel_id=1, replica_groups=mesh['dp'=16,'tensor'=2] {'dp'}, dimensions={0}, use_global_device_ids=true | all-gather | bytes 34816 | tf_op jit(solution)/shard_map/all_gather | solution.py:138
  82.1 64.5 %all-gather = f32[32,8,4]{1,2,0:T(4,128)S(1)} all-gather(f32[1,8,4]{1,2,0:T(4,128)S(1)} %bitcast.309), channel_id=1, replica_groups=mesh['dp'=16,'tensor'=2] {'dp','tensor'}, dimensions={0}, use_global_device_ids=true | all-gather | bytes 4224 | tf_op jit(solution)/shard_map/all_gather | solution.py:126
  146.7 69.6 %all_gather.34 = bf16[1024,256]{1,0:T(8,128)(2,1)S(1)} all-gather(bf16[32,256]{1,0:T(8,128)(2,1)S(1)} %copy-done.52), channel_id=1, replica_groups=mesh['dp'=16,'tensor'=2] {'dp','tensor'}, dimensions={0}, use_global_device_ids=true | all-gather | bytes 540672 | tf_op jit(solution)/shard_map/all_gather | solution.py:124
  217.5 2.9 broadcast_multiply_fusion
  222.4 2.3 fusion.163
  224.8 1.4 fusion.87
  226.3 2.0 fusion.157
  228.3 4.7 fusion.156
  233.0 6.9 fusion.36
  239.9 5.6 reshape.333
  245.6 6.7 fusion.68
  252.4 2.3 fusion.88
  255.8 3.5 fusion.158
  259.4 1.9 copy-done.12
  261.3 19.7 %fusion.35 = f32[4,256,16,64]{1,3,2,0:T(8,128)S(1)} fusion(f32[4,256,16,64]{1,3,2,0:T(8,128)S(1)} %bitcast.260, f32[4,256,16,64]{1,0,3,2:T(4,128)S(1)} %copy-done.6, f32[4,256,16]{1,2,0:T(8,128)S(1)} %bitcast.279, f32[4,256,16]{1,2,0:T(8,128)S(1)} %convolution_bitcast_fusion.2, f32[4,256,256]{2,1,0:T(8,128)S(1)} %copy-done.30, ...), kind=kOutput, calls=%fused_computation.44 | convolution fusion | flops 3242196992 | bytes 13893696 | tf_op jit(solution)/shard_map/jvp(sijh,sjhp->sihp)/dot_general | solution.py:68
  281.0 2.8 copy.106
  283.8 3.0 copy.140
  286.9 10.0 %multiply_reduce_fusion.10 = (f32[1024]{0:T(1024)S(1)}, f32[1024,1024]{0,1:T(8,128)}, f32[1024,1024]{0,1:T(8,128)}) fusion(f32[1024,1024]{0,1:T(8,128)} %bitcast.255, bf16[1024,1024]{1,0:T(8,128)(2,1)} %all-gather.8.cloned.1.call-done, bf16[1024,1024]{1,0:T(8,128)(2,1)} %all-gather.12.cloned.1.call-done), kind=kOutput, calls=%fused_computation.61 | convolution fusion | flops 2154822656 | bytes 16781312 | tf_op jit(solution)/shard_map/dot_general | solution.py:147
  296.9 4.9 psum.56
  301.9 9.4 %multiply_reduce_fusion.2 = (f32[1024]{0:T(1024)}, f32[1024]{0:T(1024)S(1)}, f32[1024,1024]{0,1:T(8,128)}) fusion(f32[1024,1024]{0,1:T(8,128)} %get-tuple-element.126, f32[1024]{0:T(1024)S(1)} %fusion.133, f32[1024]{0:T(1024)S(1)} %add_rsqrt_fusion, f32[1024]{0:T(1024)S(1)} %copy-done.69, bf16[1024,1024]{1,0:T(8,128)(2,1)} %all-gather.16.cloned.1.call-done, ...), kind=kOutput, calls=%fused_computation.46 | convolution fusion | flops 2155870208 | bytes 12603392 | tf_op jit(solution)/shard_map/dot_general | solution.py:192
  311.2 4.9 psum.57
  316.2 11.7 %multiply_reduce_fusion.3 = (f32[1024]{0:T(1024)}, f32[1024,1024]{0,1:T(8,128)}, bf16[1024,1024]{0,1:T(8,128)(2,1)}) fusion(f32[1024,1024]{0,1:T(8,128)} %get-tuple-element.133, f32[1024,1024]{0,1:T(8,128)} %get-tuple-element.165, f32[1024]{0:T(1024)S(1)} %psum.57, f32[1024,1024]{0,1:T(8,128)} %get-tuple-element.126, f32[1024]{0:T(1024)S(1)} %fusion.133, ...), kind=kLoop, calls=%fused_computation.47 | loop fusion | flops 26213376 | bytes 27283456 | tf_op jit(solution)/shard_map/transpose(jvp())/reduce_sum | solution.py:87
  327.8 5.7 reshape.339
  333.5 4.9 multiply_reduce_fusion.8
  338.6 7.0 fusion.79
  345.6 27.4 %fusion.8 = (f32[4,256,16]{1,2,0:T(8,128)}, f32[4,256,16]{1,2,0:T(8,128)}, f32[4,256,16]{1,2,0:T(8,128)}, f32[4,256,256]{2,1,0:T(8,128)S(1)}) fusion(f32[4,256,16]{1,2,0:T(8,128)S(1)} %bitcast.280, f32[4,256,16]{1,2,0:T(8,128)S(1)} %convolution_bitcast_fusion.2, f32[4,256,256]{2,1,0:T(8,128)S(1)} %copy-done.31, pred[256,256]{1,0:T(8,128)(4,1)S(1)} %copy-done.34, ...), kind=kOutput, calls=%fused_computation.11 | convolution fusion | flops 3275440128 | bytes 10878976 | tf_op jit(solution)/shard_map/transpose(jvp(sijh,sjhp->sihp))/dot_general | solution.py:68
  373.0 4.2 fusion.71
  377.3 3.1 fusion.93
  380.4 1.5 add_multiply_fusion
  381.9 6.8 fusion.74
  388.7 4.0 fusion.62
  392.7 3.7 multiply_reduce_fusion.1
  396.5 15.7 %bitcast_add_fusion = f32[4,256,16,64]{1,3,2,0:T(8,128)S(1)} fusion(f32[4,256,16,64]{1,3,2,0:T(8,128)S(1)} %fusion.62, f32[4,256,16,64]{1,0,3,2:T(4,128)S(1)} %copy-done.9, f32[4,256,16]{1,2,0:T(8,128)S(1)} %bitcast.281, f32[4,256,16]{1,2,0:T(8,128)S(1)} %convolution_bitcast_fusion.2, f32[4,256,256]{2,1,0:T(8,128)S(1)} %copy-done.31, ...), kind=kOutput, calls=%fused_computation.39 | convolution fusion | flops 3242196992 | bytes 13893696 | tf_op jit(solution)/shard_map/transpose(jvp(sijh,sjhp->sihp))/dot_general | solution.py:68
  413.3 1.9 convolution_add_fusion
  415.2 2.3 fusion.144
  418.9 2.8 copy.110
  423.9 1.3 copy-done.8
  425.2 6.4 fusion.143
  431.6 3.3 fusion.29
  434.9 3.4 fusion.30
  438.3 1.2 fusion.86
  439.6 3.4 fusion.31
  445.9 1.7 add_convert_fusion.1
  448.6 1.3 copy-done.11
  449.9 4.6 add_convert_fusion
  454.6 2.4 fusion.159
  457.0 2.4 fusion.160
  459.4 2.9 add_add_fusion
  463.0 7.5 convolution_convert_fusion
  470.8 10.8 %fusion.21 = f32[1024,2064]{1,0:T(8,128)} fusion(bf16[1024,1024]{1,0:T(8,128)(2,1)} %all-gather.8.cloned.1.call-done, bf16[1024,16]{0,1:T(8,128)(2,1)S(1)} %get-tuple-element.117, bf16[1024,1024]{0,1:T(8,128)(2,1)} %copy-done.18, bf16[1024,1024]{0,1:T(8,128)(2,1)S(1)} %copy-done.17), kind=kOutput, calls=%fused_computation.25 | convolution fusion | flops 4341202944 | bytes 14778368 | tf_op jit(solution)/shard_map/dot_general | solution.py:98
  483.3 1.7 fusion.161
  485.1 7.2 convolution_bitcast_fusion
  492.4 5.4 copy.130
  498.8 57.7 %all-reduce.36 = (f32[1024,4]{0,1:T(4,128)}, f32[1024]{0:T(1024)}, f32[16]{0:T(128)}, f32[16]{0:T(128)}, f32[16]{0:T(128)}, /*index=5*/f32[1024]{0:T(1024)}) all-reduce(f32[1024,4]{0,1:T(4,128)S(1)} %pad_add_fusion.3, f32[1024]{0:T(1024)S(1)} %copy-done.45, ...), channel_id=1, replica_groups=mesh['dp'=16,'tensor'=2] {'dp'}, use_global_device_ids=true, to_apply=%region_26.27 | all-reduce | flops 6192 | bytes 49536 | tf_op jit(solution)/shard_map/psum | solution.py:231
  556.5 2.4 multiply_reduce_fusion.11
  558.9 38.5 %all-reduce.34 = (f32[1024]{0:T(1024)S(1)}, f32[256,4]{0,1:T(4,128)S(1)}, f32[256]{0:T(256)S(1)}) all-reduce(f32[1024]{0:T(1024)S(1)} %get-tuple-element.86, f32[256,4]{0,1:T(4,128)S(1)} %pad_add_fusion.4, f32[256]{0:T(256)S(1)} %copy-done.71), channel_id=4, replica_groups=mesh['dp'=16,'tensor'=2] {'dp','tensor'}, use_global_device_ids=true, to_apply=%region_18.19.clone | all-reduce | flops 2304 | bytes 18432
  599.2 5.2 multiply_add_fusion.1
  604.4 54.9 %reduce-scatter.13.cloned.1.call-done = f32[64,2064]{1,0:T(8,128)} async-done(((f32[1024,2064]{1,0:T(8,128)}), f32[64,2064]{1,0:T(8,128)}) %reduce-scatter.13.cloned.1.call-update) | async-done | bytes 528400 | tf_op jit(solution)/shard_map/reduce_scatter | solution.py:207
  660.8 1.9 fusion.151
  662.7 135.7 %reduce-scatter.15.cloned.1.call-done = f32[32,256]{1,0:T(8,128)} async-done(((f32[1024,256]{1,0:T(8,128)}), f32[32,256]{1,0:T(8,128)}) %reduce-scatter.15.cloned.1.call-update) | async-done | bytes 32784 | tf_op jit(solution)/shard_map/reduce_scatter | solution.py:226
  798.4 73.2 %reduce-scatter.17.cloned.1.call-done = f32[64,1024]{1,0:T(8,128)} async-done(((f32[1024,1024]{1,0:T(8,128)}), f32[64,1024]{1,0:T(8,128)}) %reduce-scatter.17.cloned.1.call-update) | async-done | bytes 262160
  (277 shorter events, 25.9 us)
Async XLA Ops:
  7.2 53.0 %copy-start = (s32[4]{0:T(128)S(1)}, s32[4]{0:T(128)}, u32[]{:S(2)}) copy-start(s32[4]{0:T(128)} %param.34) | copy-start | bytes 52
  7.2 50.2 %copy-start.15 = (f32[512,1024]{1,0:T(8,128)S(1)}, f32[512,1024]{1,0:T(8,128)}, u32[]{:S(2)}) copy-start(f32[512,1024]{1,0:T(8,128)} %param.35) | copy-start | bytes 6291460
  7.2 210.3 %all-gather.8.cloned.1.call-start = ((), (), s32[]{:S(2)}) async-start(), calls=%async_computation.5 | async-start | bytes 3145728 | tf_op jit(solution)/shard_map/all_gather | solution.py:134
  9.2 49.4 %copy-start.40 = (f32[512]{0:T(512)}, f32[512]{0:T(512)S(1)}, u32[]{:S(2)}) copy-start(f32[512]{0:T(512)S(1)} %add_rsqrt_fusion.1) | copy-start | bytes 6148
  53.0 5.6 copy-start.38
  53.0 6.3 copy-start.83
  53.0 7.1 copy-start.95
  53.0 7.5 copy-start.53
  53.0 7.5 copy-start.76
  53.0 29.1 %copy-start.81 = (f32[8,4]{0,1:T(4,128)S(1)}, f32[8,4]{0,1:T(4,128)}, u32[]{:S(2)}) copy-start(f32[8,4]{0,1:T(4,128)} %param.27) | copy-start | bytes 388
  53.0 93.7 %copy-start.52 = (bf16[32,256]{1,0:T(8,128)(2,1)S(1)}, bf16[32,256]{1,0:T(8,128)(2,1)}, u32[]{:S(2)}) copy-start(bf16[32,256]{1,0:T(8,128)(2,1)} %param.23) | copy-start | bytes 49156
  55.9 161.7 %copy-start.88 = (f32[16]{0:T(128)S(1)}, f32[16]{0:T(128)}, u32[]{:S(2)}) copy-start(f32[16]{0:T(128)} %param.31) | copy-start | bytes 196
  55.9 172.4 %all-gather.10.cloned.1.call-start = ((), (), s32[]{:S(2)}) async-start(), calls=%async_computation.6 | async-start | bytes 2228224 | tf_op jit(solution)/shard_map/all_gather | solution.py:137
  56.6 230.2 %all-gather.12.cloned.1.call-start = ((), (), s32[]{:S(2)}) async-start(), calls=%async_computation.7 | async-start | bytes 2228224 | tf_op jit(solution)/shard_map/all_gather | solution.py:136
  57.4 244.5 %all-gather.16.cloned.1.call-start = ((), (), s32[]{:S(2)}) async-start(), calls=%async_computation.10 | async-start | bytes 3145728 | tf_op jit(solution)/shard_map/all_gather | solution.py:190
  58.6 243.2 %all-gather.14.cloned.1.call-start = ((), (), s32[]{:S(2)}) async-start(), calls=%async_computation.8 | async-start | bytes 2228224 | tf_op jit(solution)/shard_map/all_gather | solution.py:139
  59.2 497.3 %reduce-scatter.11.cloned.1.call-start = ((), (), s32[]{:S(2)}) async-start(), calls=%async_computation.11 | async-start | bytes 6291456 | tf_op jit(solution)/shard_map/reduce_scatter | solution.py:214
  60.1 199.3 %copy-start.33 = (pred[256,256]{1,0:T(8,128)(4,1)}, pred[256,256]{1,0:T(8,128)(4,1)S(1)}, u32[]{:S(2)}) copy-start(pred[256,256]{1,0:T(8,128)(4,1)S(1)} %convert_compare_fusion) | copy-start | bytes 196612
  60.1 160.3 %copy-start.84 = (f32[16]{0:T(128)}, f32[16]{0:T(128)S(1)}, u32[]{:S(2)}) copy-start(f32[16]{0:T(128)S(1)} %exponential_negate_fusion) | copy-start | bytes 196
  146.7 78.1 %copy-start.57 = (f32[256,1]{0,1:T(1,128)}, f32[256,1]{0,1:T(1,128)S(1)}, u32[]{:S(2)}) copy-start(f32[256,1]{0,1:T(1,128)S(1)} %get-tuple-element.157) | copy-start | bytes 3076
  146.7 78.1 %copy-start.58 = (f32[256,1]{0,1:T(1,128)}, f32[256,1]{0,1:T(1,128)S(1)}, u32[]{:S(2)}) copy-start(f32[256,1]{0,1:T(1,128)S(1)} %get-tuple-element.158) | copy-start | bytes 3076
  146.7 78.1 %copy-start.60 = (f32[256,1]{0,1:T(1,128)}, f32[256,1]{0,1:T(1,128)S(1)}, u32[]{:S(2)}) copy-start(f32[256,1]{0,1:T(1,128)S(1)} %get-tuple-element.159) | copy-start | bytes 3076
  146.7 78.1 %copy-start.62 = (f32[256,1]{0,1:T(1,128)}, f32[256,1]{0,1:T(1,128)S(1)}, u32[]{:S(2)}) copy-start(f32[256,1]{0,1:T(1,128)S(1)} %get-tuple-element.156) | copy-start | bytes 3076
  216.3 8.5 copy-start.21
  217.5 7.3 copy-start.86
  220.9 5.3 copy-start.42
  228.3 4.7 copy-start.78
  233.0 6.9 copy-start.2
  245.6 6.8 copy-start.54
  245.6 6.8 copy-start.64
  245.6 6.8 copy-start.67
  245.6 9.1 %copy-start.89 = (f32[4]{0:T(128)S(1)}, f32[4]{0:T(128)}, u32[]{:S(2)}) copy-start(f32[4]{0:T(128)} %pad.101.clone) | copy-start | bytes 52
  252.3 7.0 copy-start.13
  255.8 5.5 copy-start.6
  255.8 5.5 copy-start.30
  255.8 5.5 copy-start.35
  255.8 5.5 copy-start.93
  286.9 15.0 %copy-start.69 = (f32[1024]{0:T(1024)S(1)}, f32[1024]{0:T(1024)}, u32[]{:S(2)}) copy-start(f32[1024]{0:T(1024)} %param.32) | copy-start | bytes 12292
  301.8 14.3 %copy-start.46 = (f32[1024]{0:T(1024)}, f32[1024]{0:T(1024)S(1)}, u32[]{:S(2)}) copy-start(f32[1024]{0:T(1024)S(1)} %add_rsqrt_fusion) | copy-start | bytes 12292
  333.5 4.9 copy-start.9
  333.5 4.9 copy-start.25
  333.5 4.9 copy-start.27
  333.5 5.1 copy-start.29
  333.5 5.1 copy-start.90
  338.6 7.0 copy-start.7
  338.6 7.0 copy-start.31
  338.6 7.0 copy-start.34
  338.6 7.0 copy-start.36
  431.6 7.9 copy-start.4
  439.6 6.3 copy-start.16
  449.9 4.7 copy-start.92
  462.3 136.9 %reduce-scatter.9.cloned.1.call-start = ((), (), s32[]{:S(2)}) async-start(), calls=%async_computation.9 | async-start | bytes 3145728 | tf_op jit(solution)/shard_map/reduce_scatter | solution.py:186
  470.6 188.8 %reduce-scatter.13.cloned.1.call-start = ((), (), s32[]{:S(2)}) async-start(), calls=%async_computation.12 | async-start | bytes 9469952 | tf_op jit(solution)/shard_map/reduce_scatter | solution.py:207
  481.6 316.8 %reduce-scatter.15.cloned.1.call-start = ((), (), s32[]{:S(2)}) async-start(), calls=%async_computation.13 | async-start | bytes 1081344 | tf_op jit(solution)/shard_map/reduce_scatter | solution.py:226
  485.1 386.4 %reduce-scatter.17.cloned.1.call-start = ((), (), s32[]{:S(2)}) async-start(), calls=%async_computation.14 | async-start | bytes 4456448
  497.8 58.6 %copy-start.72 = (f32[256]{0:T(256)S(1)}, f32[256]{0:T(256)}, u32[]{:S(2)}) copy-start(f32[256]{0:T(256)} %get-tuple-element.97) | copy-start | bytes 3076
  497.8 58.6 %copy-start.73 = (f32[256]{0:T(256)S(1)}, f32[256]{0:T(256)}, u32[]{:S(2)}) copy-start(f32[256]{0:T(256)} %get-tuple-element.98) | copy-start | bytes 3076
  497.9 58.6 %copy-start.74 = (f32[256]{0:T(256)S(1)}, f32[256]{0:T(256)}, u32[]{:S(2)}) copy-start(f32[256]{0:T(256)} %get-tuple-element.99) | copy-start | bytes 3076
  497.9 58.6 %copy-start.75 = (f32[256]{0:T(256)S(1)}, f32[256]{0:T(256)}, u32[]{:S(2)}) copy-start(f32[256]{0:T(256)} %get-tuple-element.100) | copy-start | bytes 3076
  497.9 58.6 %copy-start.10 = (f32[512,1024]{1,0:T(8,128)S(1)}, f32[512,1024]{1,0:T(8,128)}, u32[]{:S(2)}) copy-start(f32[512,1024]{1,0:T(8,128)} %param.18) | copy-start | bytes 6291460
  497.9 58.6 %copy-start.39 = (f32[1024]{0:T(1024)S(1)}, f32[1024]{0:T(1024)}, u32[]{:S(2)}) copy-start(f32[1024]{0:T(1024)} %copy-done.38) | copy-start | bytes 12292
  497.9 58.6 %copy-start.41 = (f32[512]{0:T(512)S(1)}, f32[512]{0:T(512)}, u32[]{:S(2)}) copy-start(f32[512]{0:T(512)} %copy-done.40) | copy-start | bytes 6148
  497.9 61.0 %copy-start.71 = (f32[256]{0:T(256)S(1)}, f32[256]{0:T(256)}, u32[]{:S(2)}) copy-start(f32[256]{0:T(256)} %get-tuple-element.96) | copy-start | bytes 3076
  599.2 272.3 %copy-start.1 = (s32[4]{0:T(128)S(1)}, s32[4]{0:T(128)}, u32[]{:S(2)}) copy-start(s32[4]{0:T(128)} %param.34) | copy-start | bytes 52
  (43 other events, 106.9 us)
Sparse Core Ops, SparseCore 0:
  56.0 33.3 all-gather.7
  91.5 41.5 all-gather.9
  135.3 40.3 all-gather.11
  177.1 35.8 all-gather.15
  215.0 41.4 all-gather.13
  462.4 50.2 reduce-scatter.10
  515.6 31.8 reduce-scatter.8
  551.6 107.7 reduce-scatter.12
  662.2 136.1 reduce-scatter.14
  802.6 68.8 reduce-scatter.16
where the time goes:
time: 882 us; the launch traced here: 879 us
  blocking collectives  304 us (34%)
  waiting for transfers between devices  266 us (30%)
  matrix products  167 us (19%)
  other arithmetic  79 us (9%)
  local copies, waits for them, and re-layouts  46.7 us (5%)
  between operations  16.3 us (2%)
    reduce_scatter x1, waiting for transfers between devices, per_device(): lax.psum_scatter(g_w_bc_part, ('dp', 'tensor'), scatter_dimension=0, tile...  136 us
    unnamed x2, blocking collectives  80.5 us
    unnamed x11, waiting for transfers between devices  75.2 us
    all_gather x1, blocking collectives, per_device(): lax.all_gather(w_bc.astype(jnp.float32), ('dp', 'tensor'), axis=0, tiled=...  69.6 us
    all_gather x1, blocking collectives, per_device(): lax.all_gather(conv_bc_w, ('dp', 'tensor'), axis=0, tiled=True)  64.5 us
    dot_general x3, matrix products, scan_heads(): jnp.einsum('sijh,sjhp->sihp', mixing, inputs, precision=HIGHEST_PREC)  62.8 us
    psum x1, blocking collectives, per_device(): lax.psum((g_cxw, g_cxb, g_alog, g_skip, g_bias, g_norm_w), 'dp')  57.7 us
    reduce_scatter x1, waiting for transfers between devices, per_device(): lax.psum_scatter(dot_tn(normed, joined), 'dp', scatter_dimension=0, tiled...  54.9 us
  transfers between devices with their start and end apart: 10, of which 3 were waited for; matrix products, arithmetic and copies ran while one was open for 14% of the time, Pallas kernels for 0%

commit v1 on v0

--- a/solution.py
+++ b/solution.py
@@ -9,6 +9,27 @@
 BLOCK = 256
 EPSILON = 1e-05
 HIGHEST_PREC = lax.Precision.HIGHEST
+
+
+def in_order(parts, dim):
+    parts = jnp.moveaxis(parts, 0, dim)
+    shape = parts.shape
+    return parts.reshape(*shape[:dim], shape[dim] * shape[dim + 1], *shape[dim + 2 :])
+
+
+def doubled(x, axis):
+    size, index = (lax.axis_size(axis), lax.axis_index(axis))
+    blocks, bit = (x[None], 1)
+    while bit < size:
+        other = lax.ppermute(blocks, axis, [(i, i ^ bit) for i in range(size)])
+        low = index & bit == 0
+        blocks = jnp.concatenate([jnp.where(low, blocks, other), jnp.where(low, other, blocks)])
+        bit *= 2
+    return blocks
+
+
+def gather_by_bits(value, axis, dim):
+    return in_order(doubled(value, axis), dim)
 
 
 def shift_rows(values, lag_rows):
@@ -123,7 +144,7 @@
     bc_full, gain_full, conv_bcw_full, conv_bcb_full = (
         lax.all_gather(w_bc.astype(jnp.float32), ("dp", "tensor"), axis=0, tiled=True),
         lax.all_gather(norm_gain, ("dp", "tensor"), axis=0, tiled=True),
-        lax.all_gather(conv_bc_w, ("dp", "tensor"), axis=0, tiled=True),
+        gather_by_bits(conv_bc_w, ("dp", "tensor"), 0),
         lax.all_gather(conv_bc_b, ("dp", "tensor"), axis=0, tiled=True),
     )
     bc_weight = bc_full.astype(jnp.bfloat16)

time: 882 us -> 841 us (0.954)
  blocking collectives: 304 us -> 237 us
  waiting for transfers between devices: 266 us -> 288 us
    all_gather x1 -> x0, blocking collectives: 64.5 us -> none  [per_device(): lax.all_gather(conv_bc_w, ('dp', 'tensor'), axis=0, tiled=True)]
    all_gather x1, waiting for transfers between devices: 0.02 us -> 12.2 us  [per_device(): lax.all_gather(w_out, 'dp', axis=0, tiled=True)]
    unnamed x211 -> x210, local copies, waits for them, and re-layouts: 23.9 us -> 24.1 us
  transfers between devices with their start and end apart: 10 -> 15, of which waited for: 3 -> 7; matrix products, arithmetic and copies ran while one was open for 14% -> 15% of each run, Pallas kernels for 0% -> 0%
where the time goes in v1:
time: 841 us; the launch traced here: 837 us
  waiting for transfers between devices  288 us (34%)
  blocking collectives  237 us (28%)
  matrix products  166 us (20%)
  other arithmetic  79.5 us (9%)
  local copies, waits for them, and re-layouts  47.1 us (6%)
  between operations  16.4 us (2%)
    reduce_scatter x1, waiting for transfers between devices, per_device(): lax.psum_scatter(g_w_bc_part, ('dp', 'tensor'), scatter_dimension=0, tile...  136 us
    unnamed x2, blocking collectives  79.6 us
    unnamed x11, waiting for transfers between devices  74.4 us
    all_gather x1, blocking collectives, per_device(): lax.all_gather(w_bc.astype(jnp.float32), ('dp', 'tensor'), axis=0, tiled=...  69.1 us
    dot_general x3, matrix products, scan_heads(): jnp.einsum('sijh,sjhp->sihp', mixing, inputs, precision=HIGHEST_PREC)  62.9 us
    psum x1, blocking collectives, per_device(): lax.psum((g_cxw, g_cxb, g_alog, g_skip, g_bias, g_norm_w), 'dp')  58.7 us
    reduce_scatter x1, waiting for transfers between devices, per_device(): lax.psum_scatter(dot_tn(normed, joined), 'dp', scatter_dimension=0, tiled...  58.2 us
    unnamed x210, local copies, waits for them, and re-layouts  24.1 us
  transfers between devices with their start and end apart: 15, of which 7 were waited for; matrix products, arithmetic and copies ran while one was open for 15% of the time, Pallas kernels for 0%

profile of v1, /device:TPU:0, one launch (start us, length us, event | category | flops | bytes accessed | tf_op | source)
XLA Modules:
  0.0 837.1 jit_solution(13545724482724138806)
XLA Ops:
  7.3 1.9 multiply_reduce_fusion.13
  10.9 42.0 %all-reduce.35 = (f32[1024]{0:T(1024)S(1)}, f32[256]{0:T(256)}) all-reduce(f32[1024]{0:T(1024)S(1)} %dynamic-update-slice, f32[256]{0:T(256)S(1)} %dynamic-update-slice.1), channel_id=1, replica_groups=mesh['dp'=16,'tensor'=2] {'dp','tensor'}, use_global_device_ids=true, to_apply=%add.29 | all-reduce | flops 1280 | bytes 10240
  53.0 2.9 multiply_convert_fusion.2
  58.7 2.3 collective-permute-start
  61.4 69.1 %all_gather.31 = bf16[1024,256]{1,0:T(8,128)(2,1)S(1)} all-gather(bf16[32,256]{1,0:T(8,128)(2,1)S(1)} %copy-done.52), channel_id=1, replica_groups=mesh['dp'=16,'tensor'=2] {'dp','tensor'}, dimensions={0}, use_global_device_ids=true | all-gather | bytes 540672 | tf_op jit(solution)/shard_map/all_gather | solution.py:145
  132.6 3.0 collective-permute-done.2
  136.2 3.1 collective-permute-done.3
  139.5 19.4 %all-gather = bf16[16,64,16]{1,2,0:T(8,128)(2,1)S(1)} all-gather(bf16[1,64,16]{1,2,0:T(8,128)(2,1)S(1)} %bitcast.310), channel_id=1, replica_groups=mesh['dp'=16,'tensor'=2] {'dp'}, dimensions={0}, use_global_device_ids=true | all-gather | bytes 34816 | tf_op jit(solution)/shard_map/all_gather | solution.py:159
  160.7 2.9 broadcast_multiply_fusion
  165.5 2.3 fusion.163
  167.8 1.4 fusion.87
  169.3 2.0 fusion.157
  171.3 4.7 fusion.156
  176.0 6.9 fusion.36
  182.9 5.6 reshape.336
  188.5 6.8 fusion.68
  195.4 2.2 fusion.88
  198.9 3.5 fusion.158
  202.4 2.0 copy-done.12
  204.4 19.7 %fusion.35 = f32[4,256,16,64]{1,3,2,0:T(8,128)S(1)} fusion(f32[4,256,16,64]{1,3,2,0:T(8,128)S(1)} %bitcast.262, f32[4,256,16,64]{1,0,3,2:T(4,128)S(1)} %copy-done.6, f32[4,256,16]{1,2,0:T(8,128)S(1)} %bitcast.281, f32[4,256,16]{1,2,0:T(8,128)S(1)} %convolution_bitcast_fusion.2, f32[4,256,256]{2,1,0:T(8,128)S(1)} %copy-done.30, ...), kind=kOutput, calls=%fused_computation.44 | convolution fusion | flops 3242196992 | bytes 13893696 | tf_op jit(solution)/shard_map/jvp(sijh,sjhp->sihp)/dot_general | solution.py:89
  224.1 2.8 copy.108
  226.9 3.0 copy.142
  230.0 10.2 %multiply_reduce_fusion.10 = (f32[1024]{0:T(1024)S(1)}, f32[1024,1024]{0,1:T(8,128)}, f32[1024,1024]{0,1:T(8,128)}) fusion(f32[1024,1024]{0,1:T(8,128)} %bitcast.257, bf16[1024,1024]{1,0:T(8,128)(2,1)} %all-gather.7.cloned.1.call-done, bf16[1024,1024]{1,0:T(8,128)(2,1)} %all-gather.11.cloned.1.call-done), kind=kOutput, calls=%fused_computation.61 | convolution fusion | flops 2154822656 | bytes 16781312 | tf_op jit(solution)/shard_map/dot_general | solution.py:168
  240.1 4.9 psum.56
  245.1 12.2 %all-gather.13.cloned.1.call-done = bf16[1024,1024]{1,0:T(8,128)(2,1)} async-done(((bf16[64,1024]{1,0:T(8,128)(2,1)}), bf16[1024,1024]{1,0:T(8,128)(2,1)}) %all-gather.13.cloned.1.call-update) | async-done | bytes 2097168 | tf_op jit(solution)/shard_map/all_gather | solution.py:160
  257.3 9.4 %multiply_reduce_fusion.2 = (f32[1024]{0:T(1024)}, f32[1024]{0:T(1024)S(1)}, f32[1024,1024]{0,1:T(8,128)}) fusion(f32[1024,1024]{0,1:T(8,128)} %get-tuple-element.126, f32[1024]{0:T(1024)S(1)} %fusion.133, f32[1024]{0:T(1024)S(1)} %add_rsqrt_fusion, f32[1024]{0:T(1024)S(1)} %copy-done.69, bf16[1024,1024]{1,0:T(8,128)(2,1)} %all-gather.15.cloned.1.call-done, ...), kind=kOutput, calls=%fused_computation.46 | convolution fusion | flops 2155870208 | bytes 12603392 | tf_op jit(solution)/shard_map/dot_general | solution.py:213
  266.7 4.9 psum.57
  271.6 11.7 %multiply_reduce_fusion.3 = (f32[1024]{0:T(1024)}, f32[1024,1024]{0,1:T(8,128)}, bf16[1024,1024]{0,1:T(8,128)(2,1)}) fusion(f32[1024,1024]{0,1:T(8,128)} %get-tuple-element.133, f32[1024,1024]{0,1:T(8,128)} %get-tuple-element.175, f32[1024]{0:T(1024)S(1)} %psum.57, f32[1024,1024]{0,1:T(8,128)} %get-tuple-element.126, f32[1024]{0:T(1024)S(1)} %fusion.133, ...), kind=kLoop, calls=%fused_computation.47 | loop fusion | flops 26213376 | bytes 27283456 | tf_op jit(solution)/shard_map/transpose(jvp())/reduce_sum | solution.py:108
  283.3 5.7 reshape.343
  289.0 4.9 multiply_reduce_fusion.8
  294.1 7.0 fusion.79
  301.1 27.4 %fusion.8 = (f32[4,256,16]{1,2,0:T(8,128)}, f32[4,256,16]{1,2,0:T(8,128)}, f32[4,256,16]{1,2,0:T(8,128)}, f32[4,256,256]{2,1,0:T(8,128)S(1)}) fusion(f32[4,256,16]{1,2,0:T(8,128)S(1)} %bitcast.282, f32[4,256,16]{1,2,0:T(8,128)S(1)} %convolution_bitcast_fusion.2, f32[4,256,256]{2,1,0:T(8,128)S(1)} %copy-done.31, pred[256,256]{1,0:T(8,128)(4,1)S(1)} %copy-done.34, ...), kind=kOutput, calls=%fused_computation.11 | convolution fusion | flops 3275440128 | bytes 10878976 | tf_op jit(solution)/shard_map/transpose(jvp(sijh,sjhp->sihp))/dot_general | solution.py:89
  328.5 4.2 fusion.71
  332.8 3.0 fusion.93
  335.8 1.5 add_multiply_fusion
  337.3 6.8 fusion.74
  344.2 4.0 fusion.62
  348.2 3.7 multiply_reduce_fusion.1
  351.9 15.7 %bitcast_add_fusion = f32[4,256,16,64]{1,3,2,0:T(8,128)S(1)} fusion(f32[4,256,16,64]{1,3,2,0:T(8,128)S(1)} %fusion.62, f32[4,256,16,64]{1,0,3,2:T(4,128)S(1)} %copy-done.9, f32[4,256,16]{1,2,0:T(8,128)S(1)} %bitcast.283, f32[4,256,16]{1,2,0:T(8,128)S(1)} %convolution_bitcast_fusion.2, f32[4,256,256]{2,1,0:T(8,128)S(1)} %copy-done.31, ...), kind=kOutput, calls=%fused_computation.39 | convolution fusion | flops 3242196992 | bytes 13893696 | tf_op jit(solution)/shard_map/transpose(jvp(sijh,sjhp->sihp))/dot_general | solution.py:89
  368.7 1.9 convolution_add_fusion
  370.7 2.3 fusion.144
  374.4 2.8 copy.112
  380.6 6.4 fusion.143
  387.0 3.3 fusion.29
  390.4 3.4 fusion.30
  395.1 3.4 fusion.31
  401.5 1.7 add_convert_fusion.1
  405.5 4.6 add_convert_fusion
  410.2 2.4 fusion.159
  412.6 2.4 fusion.160
  415.0 2.9 add_add_fusion
  418.5 6.8 convolution_convert_fusion
  425.6 10.8 %fusion.21 = f32[1024,2064]{1,0:T(8,128)} fusion(bf16[1024,1024]{1,0:T(8,128)(2,1)} %all-gather.7.cloned.1.call-done, bf16[1024,16]{0,1:T(8,128)(2,1)S(1)} %get-tuple-element.117, bf16[1024,1024]{0,1:T(8,128)(2,1)} %copy-done.18, bf16[1024,1024]{0,1:T(8,128)(2,1)S(1)} %copy-done.17), kind=kOutput, calls=%fused_computation.25 | convolution fusion | flops 4341202944 | bytes 14778368 | tf_op jit(solution)/shard_map/dot_general | solution.py:119
  438.3 1.7 fusion.161
  440.1 7.3 convolution_bitcast_fusion
  447.4 5.5 copy.132
  453.9 58.7 %all-reduce.36 = (f32[1024,4]{0,1:T(4,128)}, f32[1024]{0:T(1024)}, f32[16]{0:T(128)}, f32[16]{0:T(128)}, f32[16]{0:T(128)}, /*index=5*/f32[1024]{0:T(1024)}) all-reduce(f32[1024,4]{0,1:T(4,128)S(1)} %pad_add_fusion.3, f32[1024]{0:T(1024)S(1)} %copy-done.45, ...), channel_id=1, replica_groups=mesh['dp'=16,'tensor'=2] {'dp'}, use_global_device_ids=true, to_apply=%region_26.27 | all-reduce | flops 6192 | bytes 49536 | tf_op jit(solution)/shard_map/psum | solution.py:252
  512.7 2.3 multiply_reduce_fusion.11
  514.9 37.6 %all-reduce.34 = (f32[1024]{0:T(1024)S(1)}, f32[256,4]{0,1:T(4,128)S(1)}, f32[256]{0:T(256)S(1)}) all-reduce(f32[1024]{0:T(1024)S(1)} %get-tuple-element.86, f32[256,4]{0,1:T(4,128)S(1)} %pad_add_fusion.4, f32[256]{0:T(256)S(1)} %copy-done.71), channel_id=4, replica_groups=mesh['dp'=16,'tensor'=2] {'dp','tensor'}, use_global_device_ids=true, to_apply=%region_18.19.clone | all-reduce | flops 2304 | bytes 18432
  554.4 5.2 multiply_add_fusion.1
  559.6 58.2 %reduce-scatter.13.cloned.1.call-done = f32[64,2064]{1,0:T(8,128)} async-done(((f32[1024,2064]{1,0:T(8,128)}), f32[64,2064]{1,0:T(8,128)}) %reduce-scatter.13.cloned.1.call-update) | async-done | bytes 528400 | tf_op jit(solution)/shard_map/reduce_scatter | solution.py:228
  619.2 1.9 fusion.151
  621.0 136.1 %reduce-scatter.15.cloned.1.call-done = f32[32,256]{1,0:T(8,128)} async-done(((f32[1024,256]{1,0:T(8,128)}), f32[32,256]{1,0:T(8,128)}) %reduce-scatter.15.cloned.1.call-update) | async-done | bytes 32784 | tf_op jit(solution)/shard_map/reduce_scatter | solution.py:247
  757.1 72.9 %reduce-scatter.17.cloned.1.call-done = f32[64,1024]{1,0:T(8,128)} async-done(((f32[1024,1024]{1,0:T(8,128)}), f32[64,1024]{1,0:T(8,128)}) %reduce-scatter.17.cloned.1.call-update) | async-done | bytes 262160
  (296 shorter events, 31.4 us)
Async XLA Ops:
  7.2 54.1 %copy-start = (s32[4]{0:T(128)S(1)}, s32[4]{0:T(128)}, u32[]{:S(2)}) copy-start(s32[4]{0:T(128)} %param.34) | copy-start | bytes 52
  7.2 50.2 %copy-start.15 = (f32[512,1024]{1,0:T(8,128)S(1)}, f32[512,1024]{1,0:T(8,128)}, u32[]{:S(2)}) copy-start(f32[512,1024]{1,0:T(8,128)} %param.35) | copy-start | bytes 6291460
  7.2 153.5 %all-gather.7.cloned.1.call-start = ((), (), s32[]{:S(2)}) async-start(), calls=%async_computation.5 | async-start | bytes 3145728 | tf_op jit(solution)/shard_map/all_gather | solution.py:155
  9.2 49.4 %copy-start.40 = (f32[512]{0:T(512)}, f32[512]{0:T(512)S(1)}, u32[]{:S(2)}) copy-start(f32[512]{0:T(512)S(1)} %add_rsqrt_fusion.1) | copy-start | bytes 6148
  53.0 5.6 copy-start.38
  53.0 5.7 copy-start.81
  53.0 8.1 copy-start.83
  53.0 8.4 %copy-start.53 = (f32[1024,4]{0,1:T(4,128)S(1)}, f32[1024,4]{0,1:T(4,128)}, u32[]{:S(2)}) copy-start(f32[1024,4]{0,1:T(4,128)} %param.25) | copy-start | bytes 49156
  53.0 8.4 %copy-start.52 = (bf16[32,256]{1,0:T(8,128)(2,1)S(1)}, bf16[32,256]{1,0:T(8,128)(2,1)}, u32[]{:S(2)}) copy-start(bf16[32,256]{1,0:T(8,128)(2,1)} %param.23) | copy-start | bytes 49156
  53.0 77.7 %copy-start.95 = (f32[16]{0:T(128)S(1)}, f32[16]{0:T(128)}, u32[]{:S(2)}) copy-start(f32[16]{0:T(128)} %param.29) | copy-start | bytes 196
  53.0 86.5 %copy-start.76 = (bf16[64,16]{0,1:T(8,128)(2,1)S(1)}, bf16[64,16]{0,1:T(8,128)(2,1)}, u32[]{:S(2)}) copy-start(bf16[64,16]{0,1:T(8,128)(2,1)} %param.22) | copy-start | bytes 6148
  55.9 104.8 %copy-start.88 = (f32[16]{0:T(128)S(1)}, f32[16]{0:T(128)}, u32[]{:S(2)}) copy-start(f32[16]{0:T(128)} %param.31) | copy-start | bytes 196
  55.9 115.4 %all-gather.9.cloned.1.call-start = ((), (), s32[]{:S(2)}) async-start(), calls=%async_computation.6 | async-start | bytes 2228224 | tf_op jit(solution)/shard_map/all_gather | solution.py:158
  56.6 173.3 %all-gather.11.cloned.1.call-start = ((), (), s32[]{:S(2)}) async-start(), calls=%async_computation.7 | async-start | bytes 2228224 | tf_op jit(solution)/shard_map/all_gather | solution.py:157
  57.4 187.7 %all-gather.15.cloned.1.call-start = ((), (), s32[]{:S(2)}) async-start(), calls=%async_computation.10 | async-start | bytes 3145728 | tf_op jit(solution)/shard_map/all_gather | solution.py:211
  58.6 198.7 %all-gather.13.cloned.1.call-start = ((), (), s32[]{:S(2)}) async-start(), calls=%async_computation.8 | async-start | bytes 2228224 | tf_op jit(solution)/shard_map/all_gather | solution.py:160
  58.7 71.9 %collective-permute-start = (f32[1,8,4]{1,2,0:T(4,128)S(1)}, f32[1,8,4]{1,2,0:T(4,128)S(1)}, u32[]{:S(2)}, u32[]{:S(2)}) collective-permute-start(f32[1,8,4]{1,2,0:T(4,128)S(1)} %bitcast.311), channel_id=1, source_target_pairs={{0,1},{1,0},{2,3},{3,2},{4,5},{5,4},{6,7},{7,6},{8,9},{9,8},{10,11... | collective-permute-start | bytes 392 | tf_op jit(solution)/shard_map/ppermute | solution.py:24
  61.0 451.6 %reduce-scatter.11.cloned.1.call-start = ((), (), s32[]{:S(2)}) async-start(), calls=%async_computation.11 | async-start | bytes 6291456 | tf_op jit(solution)/shard_map/reduce_scatter | solution.py:235
  130.5 37.2 %copy-start.21 = (bf16[1024,256]{1,0:T(8,128)(2,1)}, bf16[1024,256]{1,0:T(8,128)(2,1)S(1)}, u32[]{:S(2)}) copy-start(bf16[1024,256]{1,0:T(8,128)(2,1)S(1)} %all_gather.31) | copy-start | bytes 1572868
  130.6 1.2 collective-permute-start.1
  130.7 32.9 %copy-start.84 = (f32[16]{0:T(128)}, f32[16]{0:T(128)S(1)}, u32[]{:S(2)}) copy-start(f32[16]{0:T(128)S(1)} %exponential_negate_fusion) | copy-start | bytes 196
  131.8 3.7 collective-permute-start.2
  135.6 3.8 collective-permute-start.3
  139.4 21.0 %collective-permute-start.4 = (f32[16,8,4]{1,2,0:T(4,128)S(1)}, f32[16,8,4]{1,2,0:T(4,128)S(1)}, u32[]{:S(2)}, u32[]{:S(2)}) collective-permute-start(f32[16,8,4]{1,2,0:T(4,128)S(1)} %pad_maximum_fusion.2), channel_id=1, source_target_pairs={{0,16},{1,17},{2,18},{3,19},{4,20},{5,21},{6,22},{7,23},{8,24},{9,... | collective-permute-start | bytes 6152 | tf_op jit(solution)/shard_map/ppermute | solution.py:24
  160.6 7.2 copy-start.57
  160.6 7.2 copy-start.58
  160.6 7.2 copy-start.60
  160.6 7.2 copy-start.62
  160.6 7.2 copy-start.86
  164.0 5.2 copy-start.42
  164.7 30.6 %copy-start.54 = (f32[16]{0:T(128)}, f32[16]{0:T(128)S(1)}, u32[]{:S(2)}) copy-start(f32[16]{0:T(128)S(1)} %get-tuple-element.103) | copy-start | bytes 196
  164.7 30.7 %copy-start.64 = (f32[16]{0:T(128)}, f32[16]{0:T(128)S(1)}, u32[]{:S(2)}) copy-start(f32[16]{0:T(128)S(1)} %get-tuple-element.102) | copy-start | bytes 196
  164.7 30.7 %copy-start.67 = (f32[16]{0:T(128)}, f32[16]{0:T(128)S(1)}, u32[]{:S(2)}) copy-start(f32[16]{0:T(128)S(1)} %get-tuple-element.104) | copy-start | bytes 196
  176.0 6.9 copy-start.2
  188.5 9.2 %copy-start.89 = (f32[4]{0:T(128)S(1)}, f32[4]{0:T(128)}, u32[]{:S(2)}) copy-start(f32[4]{0:T(128)} %pad.101.clone) | copy-start | bytes 52
  195.4 7.0 copy-start.13
  198.9 5.5 copy-start.6
  198.9 5.5 copy-start.30
  198.9 5.5 copy-start.33
  198.9 5.5 copy-start.35
  198.9 5.5 copy-start.93
  230.0 27.3 %copy-start.69 = (f32[1024]{0:T(1024)S(1)}, f32[1024]{0:T(1024)}, u32[]{:S(2)}) copy-start(f32[1024]{0:T(1024)} %param.32) | copy-start | bytes 12292
  245.0 26.5 %copy-start.46 = (f32[1024]{0:T(1024)}, f32[1024]{0:T(1024)S(1)}, u32[]{:S(2)}) copy-start(f32[1024]{0:T(1024)S(1)} %add_rsqrt_fusion) | copy-start | bytes 12292
  289.0 5.1 copy-start.29
  289.0 5.1 copy-start.90
  294.1 7.0 copy-start.7
  294.1 7.0 copy-start.31
  294.1 7.0 copy-start.34
  294.1 7.0 copy-start.36
  387.0 8.0 copy-start.4
  395.1 6.4 copy-start.16
  417.9 136.5 %reduce-scatter.9.cloned.1.call-start = ((), (), s32[]{:S(2)}) async-start(), calls=%async_computation.9 | async-start | bytes 3145728 | tf_op jit(solution)/shard_map/reduce_scatter | solution.py:207
  425.4 192.3 %reduce-scatter.13.cloned.1.call-start = ((), (), s32[]{:S(2)}) async-start(), calls=%async_computation.12 | async-start | bytes 9469952 | tf_op jit(solution)/shard_map/reduce_scatter | solution.py:228
  436.5 320.6 %reduce-scatter.15.cloned.1.call-start = ((), (), s32[]{:S(2)}) async-start(), calls=%async_computation.13 | async-start | bytes 1081344 | tf_op jit(solution)/shard_map/reduce_scatter | solution.py:247
  440.1 390.0 %reduce-scatter.17.cloned.1.call-start = ((), (), s32[]{:S(2)}) async-start(), calls=%async_computation.14 | async-start | bytes 4456448
  453.0 59.6 %copy-start.72 = (f32[256]{0:T(256)S(1)}, f32[256]{0:T(256)}, u32[]{:S(2)}) copy-start(f32[256]{0:T(256)} %get-tuple-element.97) | copy-start | bytes 3076
  453.0 59.6 %copy-start.73 = (f32[256]{0:T(256)S(1)}, f32[256]{0:T(256)}, u32[]{:S(2)}) copy-start(f32[256]{0:T(256)} %get-tuple-element.98) | copy-start | bytes 3076
  453.0 59.6 %copy-start.74 = (f32[256]{0:T(256)S(1)}, f32[256]{0:T(256)}, u32[]{:S(2)}) copy-start(f32[256]{0:T(256)} %get-tuple-element.99) | copy-start | bytes 3076
  453.0 59.6 %copy-start.75 = (f32[256]{0:T(256)S(1)}, f32[256]{0:T(256)}, u32[]{:S(2)}) copy-start(f32[256]{0:T(256)} %get-tuple-element.100) | copy-start | bytes 3076
  453.0 59.6 %copy-start.10 = (f32[512,1024]{1,0:T(8,128)S(1)}, f32[512,1024]{1,0:T(8,128)}, u32[]{:S(2)}) copy-start(f32[512,1024]{1,0:T(8,128)} %param.18) | copy-start | bytes 6291460
  453.0 59.6 %copy-start.39 = (f32[1024]{0:T(1024)S(1)}, f32[1024]{0:T(1024)}, u32[]{:S(2)}) copy-start(f32[1024]{0:T(1024)} %copy-done.38) | copy-start | bytes 12292
  453.0 59.6 %copy-start.41 = (f32[512]{0:T(512)S(1)}, f32[512]{0:T(512)}, u32[]{:S(2)}) copy-start(f32[512]{0:T(512)} %copy-done.40) | copy-start | bytes 6148
  453.0 61.9 %copy-start.71 = (f32[256]{0:T(256)S(1)}, f32[256]{0:T(256)}, u32[]{:S(2)}) copy-start(f32[256]{0:T(256)} %get-tuple-element.96) | copy-start | bytes 3076
  554.3 275.7 %copy-start.1 = (s32[4]{0:T(128)S(1)}, s32[4]{0:T(128)}, u32[]{:S(2)}) copy-start(s32[4]{0:T(128)} %param.34) | copy-start | bytes 52
  (48 other events, 131.7 us)
Sparse Core Ops, SparseCore 0:
  56.0 37.7 all-gather.6
  95.9 42.1 all-gather.8
  140.3 40.3 all-gather.10
  182.1 31.6 all-gather.14
  215.8 41.4 all-gather.12
  418.0 53.0 reduce-scatter.10
  473.9 31.8 reduce-scatter.8
  510.0 107.7 reduce-scatter.12
  620.5 136.5 reduce-scatter.14
  761.4 68.6 reduce-scatter.16
